TPU v7x, 32 devices: a whole 2x2x4 slice. The times are simulated.
32 devices in a mesh: groups: 2 (over y), seq: 4 (over z), mp: 2 (over x), sub: 2 (over core).
Axes of the slice: x: 2, y: 2, z: 4, core: 2. Of those that a mesh axis runs over, the one named last changes fastest.
Arguments:
- seq_in: bfloat16 [4096, 1536], P(('groups', 'seq'), ('mp', 'sub')), parts along dimension 0, may hold values from -48 to 48
- conv_gain: float32 [3, 1536], replicated, may hold values from 0.1 to 1.9
- conv_weight: bfloat16 [3, 3, 1536, 1536], P(None, None, None, ('mp', 'sub')), may hold values from -0.09375 to 0.09375
- w_q: bfloat16 [1536, 1024], P(None, 'mp'), may hold values from -0.102062073 to 0.102062073
- w_k: bfloat16 [1536, 1024], P(None, 'mp'), may hold values from -0.102062073 to 0.102062073
- w_v: bfloat16 [1536, 1024], P(None, 'mp'), may hold values from -0.15625 to 0.15625
- w_o: bfloat16 [1024, 1536], P('mp'), may hold values from -0.1875 to 0.1875
Outputs:
- seq_out: bfloat16 [4096, 1536], P(('groups', 'seq', 'sub'), 'mp'), parts along dimension 0
There are 2 independent parts, one for each index of `groups`. A program takes and returns all parts, laid end to end along the dimension named above; an argument that names none is the same for every part. Nothing has to cross between parts.
All inputs are finite; a program needn't handle non-finite values.
Results may differ from a plain program's by a relative error of at most 0.015.
Values may be sent and summed in bfloat16 or wider, within the bound.
No kernel may reach another device: no remote copies, remote signals or barrier semaphores. Data moves between devices by JAX's collectives and lax.ppermute only.
A program may use at most 128 MiB of HBM per device.

v0:
```python
import math
import jax
import jax.numpy as jnp
from jax import lax
from jax.sharding import PartitionSpec as P

HEAD = 128
LAYERS = 3
BINS_DEV = 512


def passed_along(x, axis, by):
    devices = lax.axis_size(axis)
    pairs = [(i, i + by) for i in range(devices) if 0 <= i + by < devices]
    return lax.ppermute(x, axis, pairs)


def tower_section(stream_shard, gain_row, weight_taps, dilation):
    rows_here = stream_shard.shape[0]
    gathered = lax.all_gather(stream_shard, ("mp", "sub"), axis=1, tiled=True)
    widened = gathered.astype(jnp.float32)
    normed = (
        widened * lax.rsqrt(jnp.mean(widened * widened, axis=1, keepdims=True) + 1e-06) * gain_row
    )
    hidden = jax.nn.gelu(normed).astype(jnp.bfloat16)
    tap_terms = jnp.einsum("rc,jco->jro", hidden, weight_taps, preferred_element_type=jnp.float32)
    span_rows = min(dilation, rows_here)
    hop_count = max(dilation // rows_here, 1)
    lower_part = passed_along(
        tap_terms[0, rows_here - span_rows :].astype(jnp.bfloat16), "seq", hop_count
    ).astype(jnp.float32)
    upper_part = passed_along(
        tap_terms[2, :span_rows].astype(jnp.bfloat16), "seq", -hop_count
    ).astype(jnp.float32)
    before = jnp.concatenate([lower_part, tap_terms[0, : rows_here - span_rows]], axis=0)
    after = jnp.concatenate([tap_terms[2, span_rows:], upper_part], axis=0)
    return (stream_shard.astype(jnp.float32) + before + tap_terms[1] + after).astype(jnp.bfloat16)


def per_device(seq_in, conv_gain, conv_weight, w_q, w_k, w_v, w_o):
    rows_here = seq_in.shape[0]
    dilations = (BINS_DEV // 4, BINS_DEV, 2 * BINS_DEV)
    stream = seq_in
    for section_index in range(LAYERS):
        stream = tower_section(
            stream, conv_gain[section_index], conv_weight[section_index], dilations[section_index]
        )
    query_rows = rows_here // lax.axis_size("sub")
    mp_width = w_o.shape[1] // lax.axis_size("mp")
    widest = lax.all_gather(stream, ("mp", "sub"), axis=1, tiled=True)
    query_inputs = lax.dynamic_slice_in_dim(
        widest, lax.axis_index("sub") * query_rows, query_rows, 0
    )
    residual_part = lax.dynamic_slice_in_dim(
        query_inputs, lax.axis_index("mp") * mp_width, mp_width, 1
    )
    heads_here = w_q.shape[1] // HEAD
    queries = (
        jnp.dot(query_inputs, w_q, preferred_element_type=jnp.float32)
        .astype(jnp.bfloat16)
        .reshape(query_rows, heads_here, HEAD)
    )
    keys = (
        jnp.dot(query_inputs, w_k, preferred_element_type=jnp.float32)
        .astype(jnp.bfloat16)
        .reshape(query_rows, heads_here, HEAD)
    )
    values = (
        jnp.dot(query_inputs, w_v, preferred_element_type=jnp.float32)
        .astype(jnp.bfloat16)
        .reshape(query_rows, heads_here, HEAD)
    )
    score_scale = 1.0 / math.sqrt(HEAD)
    running_top = jnp.full((heads_here, query_rows), -1e30, jnp.float32)
    running_numer = jnp.zeros((query_rows, heads_here, HEAD), jnp.float32)
    key_rows = lax.all_gather(keys, ("seq", "sub"), axis=0, tiled=True)
    value_rows = lax.all_gather(values, ("seq", "sub"), axis=0, tiled=True)
    scores = (
        jnp.einsum("qhe,khe->hqk", queries, key_rows, preferred_element_type=jnp.float32)
        * score_scale
    )
    new_top = jnp.maximum(running_top, jnp.max(scores, axis=-1))
    expw = jnp.exp(scores - new_top[:, :, None])
    factor = jnp.exp(running_top - new_top)
    new_denom = jnp.sum(expw, axis=-1)
    contrib = jnp.einsum(
        "hqk,khe->qhe", expw.astype(jnp.bfloat16), value_rows, preferred_element_type=jnp.float32
    )
    new_numer = running_numer * factor.T[:, :, None] + contrib
    attended = (
        (new_numer / new_denom.T[:, :, None])
        .astype(jnp.bfloat16)
        .reshape(query_rows, heads_here * HEAD)
    )
    column_weight = lax.all_to_all(w_o, "mp", split_axis=1, concat_axis=0, tiled=True)
    every_head = lax.all_gather(attended, "mp", axis=1, tiled=True)
    shares = jnp.dot(every_head, column_weight, preferred_element_type=jnp.float32)
    return (residual_part.astype(jnp.float32) + shares).astype(jnp.bfloat16)


def solution(mesh):
    placed = (
        P(("groups", "seq"), ("mp", "sub")),
        P(),
        P(None, None, None, ("mp", "sub")),
        P(None, "mp"),
        P(None, "mp"),
        P(None, "mp"),
        P("mp", None),
    )
    return jax.shard_map(
        per_device,
        mesh=mesh,
        in_specs=placed,
        out_specs=P(("groups", "seq", "sub"), "mp"),
        check_vma=False,
    )
```

profile of v0, /device:TPU:8, one launch (start us, length us, event | category | flops | bytes accessed | tf_op | source)
XLA Modules:
  0.0 252.6 jit_solution(15815357984765979070)
XLA Ops:
  8.2 21.5 %all-gather.7.cloned.1.call-done = bf16[512,1536]{1,0:T(8,128)(2,1)} async-done(((bf16[512,384]{1,0:T(8,128)(2,1)}), bf16[512,1536]{1,0:T(8,128)(2,1)}) %all-gather.7.cloned.1.call-update) | async-done | bytes 1572880 | tf_op jit(solution)/shard_map/all_gather | solution.py:20
  31.6 5.6 %fusion.124 = (bf16[3,512,384]{2,1,0:T(8,128)(2,1)S(1)}, f32[3,512,384]{2,1,0:T(8,128)S(1)}) fusion(bf16[3,3,1536,384]{3,2,1,0:T(8,128)(2,1)} %param.9, bf16[512,1536]{1,0:T(8,128)(2,1)} %all-gather.7.cloned.1.call-done, f32[1536]{0:T(1024)S(1)} %get-tuple-element.6, f32[512]{0:T(512)S(1)} %add_rsqrt_fusion.2), kind=kOutput, calls=%fused_computation.142 | convolution fusion | flops 1821966336 | bytes 8658944 | tf_op jit(solution)/shard_map/rc,jco->jro/dot_general | solution.py:26
  37.2 3.5 %collective-permute-start = (bf16[128,384]{1,0:T(8,128)(2,1)S(1)}, bf16[128,384]{1,0:T(8,128)(2,1)S(1)}, u32[]{:S(2)}, u32[]{:S(2)}) collective-permute-start(bf16[128,384]{1,0:T(8,128)(2,1)S(1)} %get-tuple-element.15), channel_id=1, source_target_pairs={{0,4},{4,8},{8,12},{1,5},{5,9},{9,13},{2,6},{6,10},{10,14},{3,7},{... | collective-permute-start | bytes 294920 | tf_op jit(solution)/shard_map/ppermute | solution.py:15
  40.7 2.5 collective-permute-start.1
  44.2 3.1 %collective-permute-done.1 = bf16[128,384]{1,0:T(8,128)(2,1)S(1)} collective-permute-done((bf16[128,384]{1,0:T(8,128)(2,1)S(1)}, bf16[128,384]{1,0:T(8,128)(2,1)S(1)}, u32[]{:S(2)}, u32[]{:S(2)}) %collective-permute-start.1) | collective-permute-done | bytes 98336 | tf_op jit(solution)/shard_map/ppermute | solution.py:15
  48.3 18.8 %all-gather.9.cloned.1.call-done = bf16[512,1536]{1,0:T(8,128)(2,1)} async-done(((bf16[512,384]{1,0:T(8,128)(2,1)}), bf16[512,1536]{1,0:T(8,128)(2,1)}) %all-gather.9.cloned.1.call-update) | async-done | bytes 1572880 | tf_op jit(solution)/shard_map/all_gather | solution.py:20
  68.9 5.6 %fusion.125 = (bf16[3,512,384]{2,1,0:T(8,128)(2,1)S(1)}, f32[3,512,384]{2,1,0:T(8,128)S(1)}) fusion(bf16[3,3,1536,384]{3,2,1,0:T(8,128)(2,1)} %param.9, bf16[512,1536]{1,0:T(8,128)(2,1)} %all-gather.9.cloned.1.call-done, f32[1536]{0:T(1024)S(1)} %get-tuple-element.7, f32[512]{0:T(512)S(1)} %add_rsqrt_fusion.1), kind=kOutput, calls=%fused_computation.143 | convolution fusion | flops 1821966336 | bytes 8658944 | tf_op jit(solution)/shard_map/rc,jco->jro/dot_general | solution.py:26
  74.7 3.4 %collective-permute-start.2 = (bf16[512,384]{1,0:T(8,128)(2,1)S(1)}, bf16[512,384]{1,0:T(8,128)(2,1)S(1)}, u32[]{:S(2)}, u32[]{:S(2)}) collective-permute-start(bf16[512,384]{1,0:T(8,128)(2,1)S(1)} %get-tuple-element.12), channel_id=1, source_target_pairs={{0,4},{4,8},{8,12},{1,5},{5,9},{9,13},{2,6},{6,10},{10,14},{3,7},{... | collective-permute-start | bytes 1179656 | tf_op jit(solution)/shard_map/ppermute | solution.py:15
  78.1 2.5 collective-permute-start.3
  80.6 7.3 %collective-permute-done.2 = bf16[512,384]{1,0:T(8,128)(2,1)S(1)} collective-permute-done((bf16[512,384]{1,0:T(8,128)(2,1)S(1)}, bf16[512,384]{1,0:T(8,128)(2,1)S(1)}, u32[]{:S(2)}, u32[]{:S(2)}) %collective-permute-start.2) | collective-permute-done | bytes 393248 | tf_op jit(solution)/shard_map/ppermute | solution.py:15
  87.8 3.1 %collective-permute-done.3 = bf16[512,384]{1,0:T(8,128)(2,1)S(1)} collective-permute-done((bf16[512,384]{1,0:T(8,128)(2,1)S(1)}, bf16[512,384]{1,0:T(8,128)(2,1)S(1)}, u32[]{:S(2)}, u32[]{:S(2)}) %collective-permute-start.3) | collective-permute-done | bytes 393248 | tf_op jit(solution)/shard_map/ppermute | solution.py:15
  92.0 18.8 %all-gather.11.cloned.1.call-done = bf16[512,1536]{1,0:T(8,128)(2,1)} async-done(((bf16[512,384]{1,0:T(8,128)(2,1)}), bf16[512,1536]{1,0:T(8,128)(2,1)}) %all-gather.11.cloned.1.call-update) | async-done | bytes 1572880 | tf_op jit(solution)/shard_map/all_gather | solution.py:20
  112.6 5.6 %fusion.126 = (bf16[3,512,384]{2,1,0:T(8,128)(2,1)S(1)}, f32[3,512,384]{2,1,0:T(8,128)S(1)}) fusion(bf16[3,3,1536,384]{3,2,1,0:T(8,128)(2,1)} %param.9, bf16[512,1536]{1,0:T(8,128)(2,1)} %all-gather.11.cloned.1.call-done, f32[1536]{0:T(1024)S(1)} %get-tuple-element.5, f32[512]{0:T(512)S(1)} %add_rsqrt_fusion), kind=kOutput, calls=%fused_computation.144 | convolution fusion | flops 1821966336 | bytes 8658944 | tf_op jit(solution)/shard_map/rc,jco->jro/dot_general | solution.py:26
  118.4 4.3 %collective-permute-start.4 = (bf16[512,384]{1,0:T(8,128)(2,1)S(1)}, bf16[512,384]{1,0:T(8,128)(2,1)S(1)}, u32[]{:S(2)}, u32[]{:S(2)}) collective-permute-start(bf16[512,384]{1,0:T(8,128)(2,1)S(1)} %get-tuple-element.10), channel_id=1, source_target_pairs={{0,8},{4,12},{1,9},{5,13},{2,10},{6,14},{3,11},{7,15},{16,24},{20,... | collective-permute-start | bytes 1179656 | tf_op jit(solution)/shard_map/ppermute | solution.py:15
  124.0 15.8 %collective-permute-done.4 = bf16[512,384]{1,0:T(8,128)(2,1)S(1)} collective-permute-done((bf16[512,384]{1,0:T(8,128)(2,1)S(1)}, bf16[512,384]{1,0:T(8,128)(2,1)S(1)}, u32[]{:S(2)}, u32[]{:S(2)}) %collective-permute-start.4) | collective-permute-done | bytes 393248 | tf_op jit(solution)/shard_map/ppermute | solution.py:15
  140.9 22.0 %all-gather.13.cloned.1.call-done = bf16[512,1536]{1,0:T(8,128)(2,1)} async-done(((bf16[512,384]{1,0:T(8,128)(2,1)}), bf16[512,1536]{1,0:T(8,128)(2,1)}) %all-gather.13.cloned.1.call-update) | async-done | bytes 1572880 | tf_op jit(solution)/shard_map/all_gather | solution.py:50
  170.3 3.7 %all-to-all-start = ((bf16[512,2,768]{0,2,1:T(8,128)(2,1)}), bf16[512,2,768]{0,2,1:T(8,128)(2,1)S(1)}, u32[]{:S(2)}, u32[]{:S(2)}) async-start(bf16[512,2,768]{0,2,1:T(8,128)(2,1)} %bitcast.118), calls=%async_computation | async-start | bytes 3145728 | tf_op jit(solution)/shard_map/all_to_all | solution.py:95
  174.0 19.9 %all-to-all-done = bf16[512,2,768]{0,2,1:T(8,128)(2,1)S(1)} async-done(((bf16[512,2,768]{0,2,1:T(8,128)(2,1)}), bf16[512,2,768]{0,2,1:T(8,128)(2,1)S(1)}, u32[]{:S(2)}, u32[]{:S(2)}) %all-to-all-start) | async-done | bytes 1572896 | tf_op jit(solution)/shard_map/all_to_all | solution.py:95
  197.8 2.9 %multiply_reduce_fusion = (f32[4,256]{1,0:T(4,128)S(1)}, f32[4,256,2048]{2,1,0:T(8,128)S(1)}) fusion(bf16[2048,4,128]{2,0,1:T(8,128)(2,1)} %all-gather.15.cloned.1.call-done, bf16[32,4,8,128]{3,2,1,0:T(8,128)(2,1)S(1)} %fusion.85), kind=kOutput, calls=%fused_computation.1 | convolution fusion | flops 541064192 | bytes 10752000 | tf_op jit(solution)/shard_map/qhe,khe->hqk/dot_general | solution.py:79
  200.7 3.2 %copy-done.1 = f32[4,256,2048]{2,1,0:T(8,128)} copy-done((f32[4,256,2048]{2,1,0:T(8,128)}, f32[4,256,2048]{2,1,0:T(8,128)S(1)}, u32[]{:S(2)}) %copy-start.1) | copy-done | bytes 8388632
  205.6 22.7 %all-gather.17.cloned.1.call-done = bf16[2048,4,128]{0,2,1:T(8,128)(2,1)} async-done(((bf16[256,4,128]{0,2,1:T(8,128)(2,1)}), bf16[2048,4,128]{0,2,1:T(8,128)(2,1)}) %all-gather.17.cloned.1.call-update) | async-done | bytes 2097168 | tf_op jit(solution)/shard_map/all_gather | solution.py:77
  228.3 5.9 %fusion.90 = bf16[256,4,128]{0,2,1:T(8,128)(2,1)S(1)} fusion(bf16[2048,4,128]{0,2,1:T(8,128)(2,1)} %all-gather.17.cloned.1.call-done, f32[4,256,2048]{2,1,0:T(8,128)} %copy-done.1, f32[4,256]{1,0:T(4,128)S(1)} %get-tuple-element.17, f32[256,4]{0,1:T(4,128)S(1)} %bitcast.123, f32[256,4]{0,1:T(4,128)S(1)} %get-tuple-element.16), kind=kOutput, calls=%fused_computation.89 | convolution fusion | flops 543555584 | bytes 10760192 | tf_op jit(solution)/shard_map/hqk,khe->qhe/dot_general | solution.py:86
  234.2 9.1 %all_gather.27 = bf16[256,1024]{0,1:T(8,128)(2,1)S(1)} all-gather(bf16[256,512]{0,1:T(8,128)(2,1)S(1)} %bitcast.122), channel_id=1, replica_groups=mesh['groups'=2,'seq'=4,'mp'=2,'sub'=2] {'mp'}, dimensions={1}, use_global_device_ids=true | all-gather | bytes 786432 | tf_op jit(solution)/shard_map/all_gather | solution.py:96
  243.4 2.4 fusion.78
  (54 shorter events, 25.4 us)
Async XLA Ops:
  6.5 156.4 %copy-start = (bf16[1536,512]{1,0:T(8,128)(2,1)S(1)}, bf16[1536,512]{1,0:T(8,128)(2,1)}, u32[]{:S(2)}) copy-start(bf16[1536,512]{1,0:T(8,128)(2,1)} %param.11) | copy-start | bytes 4718596
  6.5 23.2 %all-gather.7.cloned.1.call-start = ((), (), s32[]{:S(2)}) async-start(), calls=%async_computation.1 | async-start | bytes 1966080 | tf_op jit(solution)/shard_map/all_gather | solution.py:20
  7.3 59.9 %all-gather.9.cloned.1.call-start = ((), (), s32[]{:S(2)}) async-start(), calls=%async_computation.2 | async-start | bytes 1966080 | tf_op jit(solution)/shard_map/all_gather | solution.py:20
  37.1 10.1 %copy-start.6 = (bf16[512,384]{1,0:T(8,128)(2,1)S(1)}, bf16[512,384]{1,0:T(8,128)(2,1)}, u32[]{:S(2)}) copy-start(bf16[512,384]{1,0:T(8,128)(2,1)} %param.7) | copy-start | bytes 1179652
  37.2 7.0 %collective-permute-start = (bf16[128,384]{1,0:T(8,128)(2,1)S(1)}, bf16[128,384]{1,0:T(8,128)(2,1)S(1)}, u32[]{:S(2)}, u32[]{:S(2)}) collective-permute-start(bf16[128,384]{1,0:T(8,128)(2,1)S(1)} %get-tuple-element.15), channel_id=1, source_target_pairs={{0,4},{4,8},{8,12},{1,5},{5,9},{9,13},{2,6},{6,10},{10,14},{3,7},{... | collective-permute-start | bytes 294920 | tf_op jit(solution)/shard_map/ppermute | solution.py:15
  40.7 6.6 %collective-permute-start.1 = (bf16[128,384]{1,0:T(8,128)(2,1)S(1)}, bf16[128,384]{1,0:T(8,128)(2,1)S(1)}, u32[]{:S(2)}, u32[]{:S(2)}) collective-permute-start(bf16[128,384]{1,0:T(8,128)(2,1)S(1)} %get-tuple-element.14), channel_id=1, source_target_pairs={{4,0},{8,4},{12,8},{5,1},{9,5},{13,9},{6,2},{10,6},{14,10},{7,3},{... | collective-permute-start | bytes 294920 | tf_op jit(solution)/shard_map/ppermute | solution.py:15
  48.3 62.5 %all-gather.11.cloned.1.call-start = ((), (), s32[]{:S(2)}) async-start(), calls=%async_computation.3 | async-start | bytes 1966080 | tf_op jit(solution)/shard_map/all_gather | solution.py:20
  68.9 22.0 %copy-start.3 = (bf16[512,384]{1,0:T(8,128)(2,1)S(1)}, bf16[512,384]{1,0:T(8,128)(2,1)}, u32[]{:S(2)}) copy-start(bf16[512,384]{1,0:T(8,128)(2,1)} %fusion.101) | copy-start | bytes 1179652
  74.7 13.1 %collective-permute-start.2 = (bf16[512,384]{1,0:T(8,128)(2,1)S(1)}, bf16[512,384]{1,0:T(8,128)(2,1)S(1)}, u32[]{:S(2)}, u32[]{:S(2)}) collective-permute-start(bf16[512,384]{1,0:T(8,128)(2,1)S(1)} %get-tuple-element.12), channel_id=1, source_target_pairs={{0,4},{4,8},{8,12},{1,5},{5,9},{9,13},{2,6},{6,10},{10,14},{3,7},{... | collective-permute-start | bytes 1179656 | tf_op jit(solution)/shard_map/ppermute | solution.py:15
  78.1 12.9 %collective-permute-start.3 = (bf16[512,384]{1,0:T(8,128)(2,1)S(1)}, bf16[512,384]{1,0:T(8,128)(2,1)S(1)}, u32[]{:S(2)}, u32[]{:S(2)}) collective-permute-start(bf16[512,384]{1,0:T(8,128)(2,1)S(1)} %get-tuple-element.13), channel_id=1, source_target_pairs={{4,0},{8,4},{12,8},{5,1},{9,5},{13,9},{6,2},{10,6},{14,10},{7,3},{... | collective-permute-start | bytes 1179656 | tf_op jit(solution)/shard_map/ppermute | solution.py:15
  91.9 71.0 %all-gather.13.cloned.1.call-start = ((), (), s32[]{:S(2)}) async-start(), calls=%async_computation.4 | async-start | bytes 1966080 | tf_op jit(solution)/shard_map/all_gather | solution.py:50
  112.6 27.2 %copy-start.4 = (bf16[512,384]{1,0:T(8,128)(2,1)S(1)}, bf16[512,384]{1,0:T(8,128)(2,1)}, u32[]{:S(2)}) copy-start(bf16[512,384]{1,0:T(8,128)(2,1)} %fusion.98) | copy-start | bytes 1179652
  118.4 21.5 %collective-permute-start.4 = (bf16[512,384]{1,0:T(8,128)(2,1)S(1)}, bf16[512,384]{1,0:T(8,128)(2,1)S(1)}, u32[]{:S(2)}, u32[]{:S(2)}) collective-permute-start(bf16[512,384]{1,0:T(8,128)(2,1)S(1)} %get-tuple-element.10), channel_id=1, source_target_pairs={{0,8},{4,12},{1,9},{5,13},{2,10},{6,14},{3,11},{7,15},{16,24},{20,... | collective-permute-start | bytes 1179656 | tf_op jit(solution)/shard_map/ppermute | solution.py:15
  122.7 17.1 %collective-permute-start.5 = (bf16[512,384]{1,0:T(8,128)(2,1)S(1)}, bf16[512,384]{1,0:T(8,128)(2,1)S(1)}, u32[]{:S(2)}, u32[]{:S(2)}) collective-permute-start(bf16[512,384]{1,0:T(8,128)(2,1)S(1)} %get-tuple-element.11), channel_id=1, source_target_pairs={{8,0},{12,4},{9,1},{13,5},{10,2},{14,6},{11,3},{15,7},{24,16},{28,... | collective-permute-start | bytes 1179656 | tf_op jit(solution)/shard_map/ppermute | solution.py:15
  140.8 57.0 %all-gather.15.cloned.1.call-start = ((), (), s32[]{:S(2)}) async-start(), calls=%async_computation.5 | async-start | bytes 2359296 | tf_op jit(solution)/shard_map/all_gather | solution.py:76
  140.9 27.8 %copy-start.5 = (bf16[512,1536]{1,0:T(8,128)(2,1)S(1)}, bf16[512,1536]{1,0:T(8,128)(2,1)}, u32[]{:S(2)}) copy-start(bf16[512,1536]{1,0:T(8,128)(2,1)} %param.13) | copy-start | bytes 4718596
  165.4 62.9 %all-gather.17.cloned.1.call-start = ((), (), s32[]{:S(2)}) async-start(), calls=%async_computation.6 | async-start | bytes 2359296 | tf_op jit(solution)/shard_map/all_gather | solution.py:77
  170.3 23.6 %all-to-all-start = ((bf16[512,2,768]{0,2,1:T(8,128)(2,1)}), bf16[512,2,768]{0,2,1:T(8,128)(2,1)S(1)}, u32[]{:S(2)}, u32[]{:S(2)}) async-start(bf16[512,2,768]{0,2,1:T(8,128)(2,1)} %bitcast.118), calls=%async_computation | async-start | bytes 3145728 | tf_op jit(solution)/shard_map/all_to_all | solution.py:95
  200.7 3.2 %copy-start.1 = (f32[4,256,2048]{2,1,0:T(8,128)}, f32[4,256,2048]{2,1,0:T(8,128)S(1)}, u32[]{:S(2)}) copy-start(f32[4,256,2048]{2,1,0:T(8,128)S(1)} %get-tuple-element.25) | copy-start | bytes 25165828
  228.3 15.1 %copy-start.2 = (bf16[2,512,768]{2,1,0:T(8,128)(2,1)S(1)}, bf16[2,512,768]{2,1,0:T(8,128)(2,1)}, u32[]{:S(2)}) copy-start(bf16[2,512,768]{2,1,0:T(8,128)(2,1)} %copy.18) | copy-start | bytes 4718596
Sparse Core Ops, SparseCore 0:
  8.9 20.7 all-gather.6
  48.4 18.7 all-gather.8
  92.1 18.7 all-gather.10
  140.9 21.9 all-gather.12
  165.5 29.0 all-gather.14
  196.1 32.1 all-gather.16
where the time goes:
time: 253 us
  waiting for transfers between devices  155 us (61%)
  matrix products  34.3 us (14%)
  starting transfers between devices  21.6 us (9%)
  between operations  13.7 us (5%)
  other arithmetic  9.91 us (4%)
  local copies, waits for them, and re-layouts  9.22 us (4%)
  blocking collectives  9.14 us (4%)
    all_gather x3, waiting for transfers between devices, tower_section(): gathered = lax.all_gather(stream_shard, ('mp', 'sub'), axis=1, tiled=True)  59.2 us
    ppermute x6, waiting for transfers between devices, passed_along(): return lax.ppermute(x, axis, pairs)  30.2 us
    all_gather x1, waiting for transfers between devices, per_device(): value_rows = lax.all_gather(values, ('seq', 'sub'), axis=0, tiled=True)  22.7 us
    all_gather x1, waiting for transfers between devices, per_device(): widest = lax.all_gather(stream, ('mp', 'sub'), axis=1, tiled=True)  22 us
    all_to_all x1, waiting for transfers between devices, per_device(): lax.all_to_all(w_o, 'mp', split_axis=1, concat_axis=0, tiled=True)  19.9 us
    ppermute x6, starting transfers between devices, passed_along(): return lax.ppermute(x, axis, pairs)  17.5 us
    dot_general x3, matrix products, tower_section(): jnp.einsum('rc,jco->jro', hidden, weight_taps, preferred_element_type=jnp...  16.9 us
    all_gather x1, blocking collectives, per_device(): every_head = lax.all_gather(attended, 'mp', axis=1, tiled=True)  9.14 us
  transfers between devices with their start and end apart: 13, of which 11 were waited for; matrix products, arithmetic and copies ran while one was open for 6% of the time, Pallas kernels for 0%

commit v1 on v0

--- a/solution.py
+++ b/solution.py
@@ -9,6 +9,27 @@
 BINS_DEV = 512
 
 
+def gather_around(x, axis, dim):
+    size, index, width = (lax.axis_size(axis), lax.axis_index(axis), x.shape[dim])
+    right = [(i, (i + 1) % size) for i in range(size)]
+    downward = [(i, (i - 1) % size) for i in range(size)]
+    out = jnp.zeros((*x.shape[:dim], size * width, *x.shape[dim + 1 :]), x.dtype)
+    out = lax.dynamic_update_slice_in_dim(out, x, index * width, axis=dim)
+    from_left = from_right = x
+    half = size // 2
+    for step in range(1, half + 1):
+        from_left = lax.ppermute(from_left, axis, right)
+        out = lax.dynamic_update_slice_in_dim(
+            out, from_left, (index - step) % size * width, axis=dim
+        )
+        if step < size - half:
+            from_right = lax.ppermute(from_right, axis, downward)
+            out = lax.dynamic_update_slice_in_dim(
+                out, from_right, (index + step) % size * width, axis=dim
+            )
+    return out
+
+
 def passed_along(x, axis, by):
     devices = lax.axis_size(axis)
     pairs = [(i, i + by) for i in range(devices) if 0 <= i + by < devices]
@@ -17,7 +38,7 @@
 
 def tower_section(stream_shard, gain_row, weight_taps, dilation):
     rows_here = stream_shard.shape[0]
-    gathered = lax.all_gather(stream_shard, ("mp", "sub"), axis=1, tiled=True)
+    gathered = gather_around(stream_shard, ("mp", "sub"), 1)
     widened = gathered.astype(jnp.float32)
     normed = (
         widened * lax.rsqrt(jnp.mean(widened * widened, axis=1, keepdims=True) + 1e-06) * gain_row

time: 253 us -> 228 us (0.901)
  waiting for transfers between devices: 155 us -> 131 us
  starting transfers between devices: 21.6 us -> 29.7 us
  other arithmetic: 9.91 us -> 4.24 us
  matrix products: 34.3 us -> 28.9 us
    all_gather x3 -> x0, waiting for transfers between devices: 59.2 us -> none  [tower_section(): gathered = lax.all_gather(stream_shard, ('mp', 'sub'), axis=1, tiled=True)]
    ppermute x0 -> x9, waiting for transfers between devices: none -> 34.3 us  [the longest x6 34.3 us: gather_around(): from_left = lax.ppermute(from_left, axis, right)]
    ppermute x0 -> x9, starting transfers between devices: none -> 11.5 us  [the longest x6 7.76 us: gather_around(): from_left = lax.ppermute(from_left, axis, right)]
    dot_general x3, matrix products: 16.9 us -> 11.5 us  [tower_section(): jnp.einsum('rc,jco->jro', hidden, weight_taps, preferred_element_type=jnp...]
    reduce_sum x3, other arithmetic: 5.37 us -> 1.15 us  [tower_section(): jnp.mean(widened * widened, axis=1, keepdims=True) + 1e-06]
    ppermute x6, starting transfers between devices: 17.5 us -> 14.4 us  [passed_along(): return lax.ppermute(x, axis, pairs)]
    all_gather x1, waiting for transfers between devices: 22 us -> 24.6 us  [per_device(): widest = lax.all_gather(stream, ('mp', 'sub'), axis=1, tiled=True)]
  transfers between devices with their start and end apart: 13 -> 19, of which waited for: 11 -> 14; matrix products, arithmetic and copies ran while one was open for 6% -> 7% of each run, Pallas kernels for 0% -> 0%
where the time goes in v1:
time: 228 us
  waiting for transfers between devices  131 us (57%)
  starting transfers between devices  29.7 us (13%)
  matrix products  28.9 us (13%)
  between operations  13.6 us (6%)
  local copies, waits for them, and re-layouts  11.2 us (5%)
  blocking collectives  9.14 us (4%)
  other arithmetic  4.24 us (2%)
    ppermute x6, waiting for transfers between devices, gather_around(): from_left = lax.ppermute(from_left, axis, right)  34.3 us
    ppermute x6, waiting for transfers between devices, passed_along(): return lax.ppermute(x, axis, pairs)  29 us
    all_gather x1, waiting for transfers between devices, per_device(): widest = lax.all_gather(stream, ('mp', 'sub'), axis=1, tiled=True)  24.6 us
    all_gather x1, waiting for transfers between devices, per_device(): value_rows = lax.all_gather(values, ('seq', 'sub'), axis=0, tiled=True)  23 us
    all_to_all x1, waiting for transfers between devices, per_device(): lax.all_to_all(w_o, 'mp', split_axis=1, concat_axis=0, tiled=True)  19.9 us
    ppermute x6, starting transfers between devices, passed_along(): return lax.ppermute(x, axis, pairs)  14.4 us
    dot_general x3, matrix products, tower_section(): jnp.einsum('rc,jco->jro', hidden, weight_taps, preferred_element_type=jnp...  11.5 us
    all_gather x1, blocking collectives, per_device(): every_head = lax.all_gather(attended, 'mp', axis=1, tiled=True)  9.14 us
  transfers between devices with their start and end apart: 19, of which 14 were waited for; matrix products, arithmetic and copies ran while one was open for 7% of the time, Pallas kernels for 0%

profile of v1, /device:TPU:8, one launch (start us, length us, event | category | flops | bytes accessed | tf_op | source)
XLA Modules:
  0.0 227.6 jit_solution(6798353197573981971)
XLA Ops:
  8.3 8.0 %collective-permute-done = bf16[512,384]{1,0:T(8,128)(2,1)S(1)} collective-permute-done((bf16[512,384]{1,0:T(8,128)(2,1)}, bf16[512,384]{1,0:T(8,128)(2,1)S(1)}, u32[]{:S(2)}, u32[]{:S(2)}) %collective-permute-start) | collective-permute-done | bytes 393248 | tf_op jit(solution)/shard_map/ppermute | solution.py:21
  18.9 4.6 %collective-permute-done.2 = bf16[512,384]{1,0:T(8,128)(2,1)S(1)} collective-permute-done((bf16[512,384]{1,0:T(8,128)(2,1)S(1)}, bf16[512,384]{1,0:T(8,128)(2,1)S(1)}, u32[]{:S(2)}, u32[]{:S(2)}) %collective-permute-start.2) | collective-permute-done | bytes 393248 | tf_op jit(solution)/shard_map/ppermute | solution.py:21
  24.0 5.3 %fusion.126 = (bf16[3,512,384]{2,1,0:T(8,128)(2,1)S(1)}, f32[3,512,384]{2,1,0:T(8,128)S(1)}) fusion(bf16[3,3,1536,384]{3,2,1,0:T(8,128)(2,1)} %param.9, bf16[512,1536]{1,0:T(8,128)(2,1)S(1)} %constant_dynamic-update-slice_fusion.8, f32[1536]{0:T(1024)S(1)} %get-tuple-element.6, f32[512]{0:T(512)S(1)} %add_rsqrt_fusion.2), kind=kOutput, calls=%fused_computation.154 | convolution fusion | flops 1821966336 | bytes 8658944 | tf_op jit(solution)/shard_map/rc,jco->jro/dot_general | solution.py:47
  29.3 3.6 %collective-permute-start.3 = (bf16[128,384]{1,0:T(8,128)(2,1)S(1)}, bf16[128,384]{1,0:T(8,128)(2,1)S(1)}, u32[]{:S(2)}, u32[]{:S(2)}) collective-permute-start(bf16[128,384]{1,0:T(8,128)(2,1)S(1)} %get-tuple-element.18), channel_id=1, source_target_pairs={{0,4},{4,8},{8,12},{1,5},{5,9},{9,13},{2,6},{6,10},{10,14},{3,7},{... | collective-permute-start | bytes 294920 | tf_op jit(solution)/shard_map/ppermute | solution.py:36
  36.2 3.2 %collective-permute-done.4 = bf16[128,384]{1,0:T(8,128)(2,1)S(1)} collective-permute-done((bf16[128,384]{1,0:T(8,128)(2,1)S(1)}, bf16[128,384]{1,0:T(8,128)(2,1)S(1)}, u32[]{:S(2)}, u32[]{:S(2)}) %collective-permute-start.4) | collective-permute-done | bytes 98336 | tf_op jit(solution)/shard_map/ppermute | solution.py:36
  41.6 6.8 %collective-permute-done.5 = bf16[512,384]{1,0:T(8,128)(2,1)S(1)} collective-permute-done((bf16[512,384]{1,0:T(8,128)(2,1)S(1)}, bf16[512,384]{1,0:T(8,128)(2,1)S(1)}, u32[]{:S(2)}, u32[]{:S(2)}) %collective-permute-start.5) | collective-permute-done | bytes 393248 | tf_op jit(solution)/shard_map/ppermute | solution.py:21
  51.4 4.2 %collective-permute-done.7 = bf16[512,384]{1,0:T(8,128)(2,1)S(1)} collective-permute-done((bf16[512,384]{1,0:T(8,128)(2,1)S(1)}, bf16[512,384]{1,0:T(8,128)(2,1)S(1)}, u32[]{:S(2)}, u32[]{:S(2)}) %collective-permute-start.7) | collective-permute-done | bytes 393248 | tf_op jit(solution)/shard_map/ppermute | solution.py:21
  56.1 3.1 %fusion.127 = (bf16[3,512,384]{2,1,0:T(8,128)(2,1)S(1)}, f32[3,512,384]{2,1,0:T(8,128)S(1)}) fusion(bf16[3,3,1536,384]{3,2,1,0:T(8,128)(2,1)S(1)} %bitcast.128, bf16[512,1536]{1,0:T(8,128)(2,1)S(1)} %constant_dynamic-update-slice_fusion.4, f32[1536]{0:T(1024)S(1)} %get-tuple-element.7, f32[512]{0:T(512)S(1)} %add_rsqrt_fusion.1), kind=kOutput, calls=%fused_computation.155 | convolution fusion | flops 1821966336 | bytes 8660992 | tf_op jit(solution)/shard_map/rc,jco->jro/dot_general | solution.py:47
  59.3 3.5 %collective-permute-start.8 = (bf16[512,384]{1,0:T(8,128)(2,1)S(1)}, bf16[512,384]{1,0:T(8,128)(2,1)S(1)}, u32[]{:S(2)}, u32[]{:S(2)}) collective-permute-start(bf16[512,384]{1,0:T(8,128)(2,1)S(1)} %get-tuple-element.16), channel_id=1, source_target_pairs={{0,4},{4,8},{8,12},{1,5},{5,9},{9,13},{2,6},{6,10},{10,14},{3,7},{... | collective-permute-start | bytes 1179656 | tf_op jit(solution)/shard_map/ppermute | solution.py:36
  65.2 6.0 %collective-permute-done.8 = bf16[512,384]{1,0:T(8,128)(2,1)S(1)} collective-permute-done((bf16[512,384]{1,0:T(8,128)(2,1)S(1)}, bf16[512,384]{1,0:T(8,128)(2,1)S(1)}, u32[]{:S(2)}, u32[]{:S(2)}) %collective-permute-start.8) | collective-permute-done | bytes 393248 | tf_op jit(solution)/shard_map/ppermute | solution.py:36
  71.2 3.8 %collective-permute-done.9 = bf16[512,384]{1,0:T(8,128)(2,1)S(1)} collective-permute-done((bf16[512,384]{1,0:T(8,128)(2,1)S(1)}, bf16[512,384]{1,0:T(8,128)(2,1)S(1)}, u32[]{:S(2)}, u32[]{:S(2)}) %collective-permute-start.9) | collective-permute-done | bytes 393248 | tf_op jit(solution)/shard_map/ppermute | solution.py:36
  77.2 6.6 %collective-permute-done.10 = bf16[512,384]{1,0:T(8,128)(2,1)S(1)} collective-permute-done((bf16[512,384]{1,0:T(8,128)(2,1)S(1)}, bf16[512,384]{1,0:T(8,128)(2,1)S(1)}, u32[]{:S(2)}, u32[]{:S(2)}) %collective-permute-start.10) | collective-permute-done | bytes 393248 | tf_op jit(solution)/shard_map/ppermute | solution.py:21
  83.8 3.0 %collective-permute-start.12 = (bf16[512,384]{1,0:T(8,128)(2,1)S(1)}, bf16[512,384]{1,0:T(8,128)(2,1)S(1)}, u32[]{:S(2)}, u32[]{:S(2)}) collective-permute-start(bf16[512,384]{1,0:T(8,128)(2,1)S(1)} %collective-permute-done.10), channel_id=1, source_target_pairs={{0,1},{1,2},{2,3},{3,0},{4,5},{5,6},{6,7},{7,4},{8,9},{9,10},{10,1... | collective-permute-start | bytes 1179656 | tf_op jit(solution)/shard_map/ppermute | solution.py:21
  86.9 4.1 %collective-permute-done.12 = bf16[512,384]{1,0:T(8,128)(2,1)S(1)} collective-permute-done((bf16[512,384]{1,0:T(8,128)(2,1)S(1)}, bf16[512,384]{1,0:T(8,128)(2,1)S(1)}, u32[]{:S(2)}, u32[]{:S(2)}) %collective-permute-start.12) | collective-permute-done | bytes 393248 | tf_op jit(solution)/shard_map/ppermute | solution.py:21
  91.5 3.1 %fusion.128 = (bf16[3,512,384]{2,1,0:T(8,128)(2,1)S(1)}, f32[3,512,384]{2,1,0:T(8,128)S(1)}) fusion(bf16[3,3,1536,384]{3,2,1,0:T(8,128)(2,1)S(1)} %bitcast.128, bf16[512,1536]{1,0:T(8,128)(2,1)S(1)} %constant_dynamic-update-slice_fusion, f32[1536]{0:T(1024)S(1)} %get-tuple-element.5, f32[512]{0:T(512)S(1)} %add_rsqrt_fusion), kind=kOutput, calls=%fused_computation.156 | convolution fusion | flops 1821966336 | bytes 8660992 | tf_op jit(solution)/shard_map/rc,jco->jro/dot_general | solution.py:47
  97.4 15.2 %collective-permute-done.13 = bf16[512,384]{1,0:T(8,128)(2,1)S(1)} collective-permute-done((bf16[512,384]{1,0:T(8,128)(2,1)S(1)}, bf16[512,384]{1,0:T(8,128)(2,1)S(1)}, u32[]{:S(2)}, u32[]{:S(2)}) %collective-permute-start.13) | collective-permute-done | bytes 393248 | tf_op jit(solution)/shard_map/ppermute | solution.py:36
  113.5 24.6 %all-gather.4.cloned.1.call-done = bf16[512,1536]{1,0:T(8,128)(2,1)} async-done(((bf16[512,384]{1,0:T(8,128)(2,1)}), bf16[512,1536]{1,0:T(8,128)(2,1)}) %all-gather.4.cloned.1.call-update) | async-done | bytes 1572880 | tf_op jit(solution)/shard_map/all_gather | solution.py:71
  145.3 3.7 %all-to-all-start = ((bf16[512,2,768]{0,2,1:T(8,128)(2,1)}), bf16[512,2,768]{0,2,1:T(8,128)(2,1)S(1)}, u32[]{:S(2)}, u32[]{:S(2)}) async-start(bf16[512,2,768]{0,2,1:T(8,128)(2,1)} %bitcast.121), calls=%async_computation | async-start | bytes 3145728 | tf_op jit(solution)/shard_map/all_to_all | solution.py:116
  149.0 19.9 %all-to-all-done = bf16[512,2,768]{0,2,1:T(8,128)(2,1)S(1)} async-done(((bf16[512,2,768]{0,2,1:T(8,128)(2,1)}), bf16[512,2,768]{0,2,1:T(8,128)(2,1)S(1)}, u32[]{:S(2)}, u32[]{:S(2)}) %all-to-all-start) | async-done | bytes 1572896 | tf_op jit(solution)/shard_map/all_to_all | solution.py:116
  172.8 2.9 %multiply_reduce_fusion = (f32[4,256]{1,0:T(4,128)S(1)}, f32[4,256,2048]{2,1,0:T(8,128)S(1)}) fusion(bf16[2048,4,128]{2,0,1:T(8,128)(2,1)} %all-gather.6.cloned.1.call-done, bf16[32,4,8,128]{3,2,1,0:T(8,128)(2,1)S(1)} %fusion.85), kind=kOutput, calls=%fused_computation.1 | convolution fusion | flops 541064192 | bytes 10752000 | tf_op jit(solution)/shard_map/qhe,khe->hqk/dot_general | solution.py:100
  175.7 3.2 %copy-done.1 = f32[4,256,2048]{2,1,0:T(8,128)} copy-done((f32[4,256,2048]{2,1,0:T(8,128)}, f32[4,256,2048]{2,1,0:T(8,128)S(1)}, u32[]{:S(2)}) %copy-start.1) | copy-done | bytes 8388632
  180.6 23.0 %all-gather.8.cloned.1.call-done = bf16[2048,4,128]{0,2,1:T(8,128)(2,1)} async-done(((bf16[256,4,128]{0,2,1:T(8,128)(2,1)}), bf16[2048,4,128]{0,2,1:T(8,128)(2,1)}) %all-gather.8.cloned.1.call-update) | async-done | bytes 2097168 | tf_op jit(solution)/shard_map/all_gather | solution.py:98
  203.6 5.9 %fusion.90 = bf16[256,4,128]{0,2,1:T(8,128)(2,1)S(1)} fusion(bf16[2048,4,128]{0,2,1:T(8,128)(2,1)} %all-gather.8.cloned.1.call-done, f32[4,256,2048]{2,1,0:T(8,128)} %copy-done.1, f32[4,256]{1,0:T(4,128)S(1)} %get-tuple-element.21, f32[256,4]{0,1:T(4,128)S(1)} %bitcast.126, f32[256,4]{0,1:T(4,128)S(1)} %get-tuple-element.20), kind=kOutput, calls=%fused_computation.89 | convolution fusion | flops 543555584 | bytes 10760192 | tf_op jit(solution)/shard_map/hqk,khe->qhe/dot_general | solution.py:107
  209.6 9.1 %all_gather.15 = bf16[256,1024]{0,1:T(8,128)(2,1)S(1)} all-gather(bf16[256,512]{0,1:T(8,128)(2,1)S(1)} %bitcast.125), channel_id=1, replica_groups=mesh['groups'=2,'seq'=4,'mp'=2,'sub'=2] {'mp'}, dimensions={1}, use_global_device_ids=true | all-gather | bytes 786432 | tf_op jit(solution)/shard_map/all_gather | solution.py:117
  (79 shorter events, 37.5 us)
Async XLA Ops:
  6.5 131.6 %copy-start = (bf16[1536,512]{1,0:T(8,128)(2,1)S(1)}, bf16[1536,512]{1,0:T(8,128)(2,1)}, u32[]{:S(2)}) copy-start(bf16[1536,512]{1,0:T(8,128)(2,1)} %param.11) | copy-start | bytes 4718596
  6.5 131.6 %all-gather.4.cloned.1.call-start = ((), (), s32[]{:S(2)}) async-start(), calls=%async_computation.1 | async-start | bytes 1966080 | tf_op jit(solution)/shard_map/all_gather | solution.py:71
  6.5 9.8 %collective-permute-start = (bf16[512,384]{1,0:T(8,128)(2,1)}, bf16[512,384]{1,0:T(8,128)(2,1)S(1)}, u32[]{:S(2)}, u32[]{:S(2)}) collective-permute-start(bf16[512,384]{1,0:T(8,128)(2,1)} %param.7), channel_id=1, source_target_pairs={{0,1},{1,2},{2,3},{3,0},{4,5},{5,6},{6,7},{7,4},{8,9},{9,10},{10,1... | collective-permute-start | bytes 1179656 | tf_op jit(solution)/shard_map/ppermute | solution.py:21
  6.5 12.3 %collective-permute-start.1 = (bf16[512,384]{1,0:T(8,128)(2,1)}, bf16[512,384]{1,0:T(8,128)(2,1)S(1)}, u32[]{:S(2)}, u32[]{:S(2)}) collective-permute-start(bf16[512,384]{1,0:T(8,128)(2,1)} %param.7), channel_id=1, source_target_pairs={{0,3},{1,0},{2,1},{3,2},{4,7},{5,4},{6,5},{7,6},{8,11},{9,8},{10,9... | collective-permute-start | bytes 1179656 | tf_op jit(solution)/shard_map/ppermute | solution.py:26
  16.3 7.2 %collective-permute-start.2 = (bf16[512,384]{1,0:T(8,128)(2,1)S(1)}, bf16[512,384]{1,0:T(8,128)(2,1)S(1)}, u32[]{:S(2)}, u32[]{:S(2)}) collective-permute-start(bf16[512,384]{1,0:T(8,128)(2,1)S(1)} %collective-permute-done), channel_id=1, source_target_pairs={{0,1},{1,2},{2,3},{3,0},{4,5},{5,6},{6,7},{7,4},{8,9},{9,10},{10,1... | collective-permute-start | bytes 1179656 | tf_op jit(solution)/shard_map/ppermute | solution.py:21
  24.0 32.1 %slice-start = ((s8[10616832]{0:T(1024)(128)(4,1)}), s8[4194304]{0:T(1024)(128)(4,1)S(1)}, s32[]{:S(2)}) async-start(s8[10616832]{0:T(1024)(128)(4,1)} %bitcast.127), calls=%async_computation.4 | async-start | bytes 8388608
  24.0 32.1 %slice-start.1 = ((s8[10616832]{0:T(1024)(128)(4,1)}), s8[4194304]{0:T(1024)(128)(4,1)S(1)}, s32[]{:S(2)}) async-start(s8[10616832]{0:T(1024)(128)(4,1)} %bitcast.127), calls=%async_computation.5 | async-start | bytes 8388608
  29.3 6.9 %collective-permute-start.3 = (bf16[128,384]{1,0:T(8,128)(2,1)S(1)}, bf16[128,384]{1,0:T(8,128)(2,1)S(1)}, u32[]{:S(2)}, u32[]{:S(2)}) collective-permute-start(bf16[128,384]{1,0:T(8,128)(2,1)S(1)} %get-tuple-element.18), channel_id=1, source_target_pairs={{0,4},{4,8},{8,12},{1,5},{5,9},{9,13},{2,6},{6,10},{10,14},{3,7},{... | collective-permute-start | bytes 294920 | tf_op jit(solution)/shard_map/ppermute | solution.py:36
  32.9 6.5 %collective-permute-start.4 = (bf16[128,384]{1,0:T(8,128)(2,1)S(1)}, bf16[128,384]{1,0:T(8,128)(2,1)S(1)}, u32[]{:S(2)}, u32[]{:S(2)}) collective-permute-start(bf16[128,384]{1,0:T(8,128)(2,1)S(1)} %get-tuple-element.19), channel_id=1, source_target_pairs={{4,0},{8,4},{12,8},{5,1},{9,5},{13,9},{6,2},{10,6},{14,10},{7,3},{... | collective-permute-start | bytes 294920 | tf_op jit(solution)/shard_map/ppermute | solution.py:36
  35.3 20.8 %slice-start.2 = ((s8[10616832]{0:T(1024)(128)(4,1)}), s8[2228224]{0:T(1024)(128)(4,1)S(1)}, s32[]{:S(2)}) async-start(s8[10616832]{0:T(1024)(128)(4,1)} %bitcast.127), calls=%async_computation.6 | async-start | bytes 4456448
  39.8 8.6 %collective-permute-start.5 = (bf16[512,384]{1,0:T(8,128)(2,1)S(1)}, bf16[512,384]{1,0:T(8,128)(2,1)S(1)}, u32[]{:S(2)}, u32[]{:S(2)}) collective-permute-start(bf16[512,384]{1,0:T(8,128)(2,1)S(1)} %get-tuple-element.11), channel_id=1, source_target_pairs={{0,1},{1,2},{2,3},{3,0},{4,5},{5,6},{6,7},{7,4},{8,9},{9,10},{10,1... | collective-permute-start | bytes 1179656 | tf_op jit(solution)/shard_map/ppermute | solution.py:21
  39.9 11.4 %collective-permute-start.6 = (bf16[512,384]{1,0:T(8,128)(2,1)S(1)}, bf16[512,384]{1,0:T(8,128)(2,1)S(1)}, u32[]{:S(2)}, u32[]{:S(2)}) collective-permute-start(bf16[512,384]{1,0:T(8,128)(2,1)S(1)} %get-tuple-element.11), channel_id=1, source_target_pairs={{0,3},{1,0},{2,1},{3,2},{4,7},{5,4},{6,5},{7,6},{8,11},{9,8},{10,9... | collective-permute-start | bytes 1179656 | tf_op jit(solution)/shard_map/ppermute | solution.py:26
  48.4 7.2 %collective-permute-start.7 = (bf16[512,384]{1,0:T(8,128)(2,1)S(1)}, bf16[512,384]{1,0:T(8,128)(2,1)S(1)}, u32[]{:S(2)}, u32[]{:S(2)}) collective-permute-start(bf16[512,384]{1,0:T(8,128)(2,1)S(1)} %collective-permute-done.5), channel_id=1, source_target_pairs={{0,1},{1,2},{2,3},{3,0},{4,5},{5,6},{6,7},{7,4},{8,9},{9,10},{10,1... | collective-permute-start | bytes 1179656 | tf_op jit(solution)/shard_map/ppermute | solution.py:21
  59.3 11.9 %collective-permute-start.8 = (bf16[512,384]{1,0:T(8,128)(2,1)S(1)}, bf16[512,384]{1,0:T(8,128)(2,1)S(1)}, u32[]{:S(2)}, u32[]{:S(2)}) collective-permute-start(bf16[512,384]{1,0:T(8,128)(2,1)S(1)} %get-tuple-element.16), channel_id=1, source_target_pairs={{0,4},{4,8},{8,12},{1,5},{5,9},{9,13},{2,6},{6,10},{10,14},{3,7},{... | collective-permute-start | bytes 1179656 | tf_op jit(solution)/shard_map/ppermute | solution.py:36
  62.8 12.2 %collective-permute-start.9 = (bf16[512,384]{1,0:T(8,128)(2,1)S(1)}, bf16[512,384]{1,0:T(8,128)(2,1)S(1)}, u32[]{:S(2)}, u32[]{:S(2)}) collective-permute-start(bf16[512,384]{1,0:T(8,128)(2,1)S(1)} %get-tuple-element.17), channel_id=1, source_target_pairs={{4,0},{8,4},{12,8},{5,1},{9,5},{13,9},{6,2},{10,6},{14,10},{7,3},{... | collective-permute-start | bytes 1179656 | tf_op jit(solution)/shard_map/ppermute | solution.py:36
  75.4 8.4 %collective-permute-start.10 = (bf16[512,384]{1,0:T(8,128)(2,1)S(1)}, bf16[512,384]{1,0:T(8,128)(2,1)S(1)}, u32[]{:S(2)}, u32[]{:S(2)}) collective-permute-start(bf16[512,384]{1,0:T(8,128)(2,1)S(1)} %get-tuple-element.9), channel_id=1, source_target_pairs={{0,1},{1,2},{2,3},{3,0},{4,5},{5,6},{6,7},{7,4},{8,9},{9,10},{10,1... | collective-permute-start | bytes 1179656 | tf_op jit(solution)/shard_map/ppermute | solution.py:21
  76.9 9.9 %collective-permute-start.11 = (bf16[512,384]{1,0:T(8,128)(2,1)S(1)}, bf16[512,384]{1,0:T(8,128)(2,1)S(1)}, u32[]{:S(2)}, u32[]{:S(2)}) collective-permute-start(bf16[512,384]{1,0:T(8,128)(2,1)S(1)} %get-tuple-element.9), channel_id=1, source_target_pairs={{0,3},{1,0},{2,1},{3,2},{4,7},{5,4},{6,5},{7,6},{8,11},{9,8},{10,9... | collective-permute-start | bytes 1179656 | tf_op jit(solution)/shard_map/ppermute | solution.py:26
  83.8 7.3 %collective-permute-start.12 = (bf16[512,384]{1,0:T(8,128)(2,1)S(1)}, bf16[512,384]{1,0:T(8,128)(2,1)S(1)}, u32[]{:S(2)}, u32[]{:S(2)}) collective-permute-start(bf16[512,384]{1,0:T(8,128)(2,1)S(1)} %collective-permute-done.10), channel_id=1, source_target_pairs={{0,1},{1,2},{2,3},{3,0},{4,5},{5,6},{6,7},{7,4},{8,9},{9,10},{10,1... | collective-permute-start | bytes 1179656 | tf_op jit(solution)/shard_map/ppermute | solution.py:21
  94.7 17.8 %collective-permute-start.13 = (bf16[512,384]{1,0:T(8,128)(2,1)S(1)}, bf16[512,384]{1,0:T(8,128)(2,1)S(1)}, u32[]{:S(2)}, u32[]{:S(2)}) collective-permute-start(bf16[512,384]{1,0:T(8,128)(2,1)S(1)} %get-tuple-element.14), channel_id=1, source_target_pairs={{0,8},{4,12},{1,9},{5,13},{2,10},{6,14},{3,11},{7,15},{16,24},{20,... | collective-permute-start | bytes 1179656 | tf_op jit(solution)/shard_map/ppermute | solution.py:36
  96.1 16.5 %collective-permute-start.14 = (bf16[512,384]{1,0:T(8,128)(2,1)S(1)}, bf16[512,384]{1,0:T(8,128)(2,1)S(1)}, u32[]{:S(2)}, u32[]{:S(2)}) collective-permute-start(bf16[512,384]{1,0:T(8,128)(2,1)S(1)} %get-tuple-element.15), channel_id=1, source_target_pairs={{8,0},{12,4},{9,1},{13,5},{10,2},{14,6},{11,3},{15,7},{24,16},{28,... | collective-permute-start | bytes 1179656 | tf_op jit(solution)/shard_map/ppermute | solution.py:36
  113.5 59.3 %all-gather.6.cloned.1.call-start = ((), (), s32[]{:S(2)}) async-start(), calls=%async_computation.2 | async-start | bytes 2359296 | tf_op jit(solution)/shard_map/all_gather | solution.py:97
  140.6 63.0 %all-gather.8.cloned.1.call-start = ((), (), s32[]{:S(2)}) async-start(), calls=%async_computation.3 | async-start | bytes 2359296 | tf_op jit(solution)/shard_map/all_gather | solution.py:98
  145.3 23.6 %all-to-all-start = ((bf16[512,2,768]{0,2,1:T(8,128)(2,1)}), bf16[512,2,768]{0,2,1:T(8,128)(2,1)S(1)}, u32[]{:S(2)}, u32[]{:S(2)}) async-start(bf16[512,2,768]{0,2,1:T(8,128)(2,1)} %bitcast.121), calls=%async_computation | async-start | bytes 3145728 | tf_op jit(solution)/shard_map/all_to_all | solution.py:116
  203.6 15.1 %copy-start.2 = (bf16[2,512,768]{2,1,0:T(8,128)(2,1)S(1)}, bf16[2,512,768]{2,1,0:T(8,128)(2,1)}, u32[]{:S(2)}) copy-start(bf16[2,512,768]{2,1,0:T(8,128)(2,1)} %copy.24) | copy-start | bytes 4718596
  (3 other events, 17.5 us)
Sparse Core Ops, SparseCore 0:
  113.6 24.4 all-gather.3
  140.7 29.0 all-gather.5
  171.4 32.1 all-gather.7
